TPU v7x, 256 devices: a whole 4x4x8 slice. The times are simulated.
256 devices in a mesh: dp: 2 (over core), ctx: 32 (over y, z), grp: 4 (over x).
Axes of the slice: x: 4, y: 4, z: 8, core: 2. Of those that a mesh axis runs over, the one named last changes fastest.
Arguments:
- projected: bfloat16 [4, 8192, 3, 4096], P('dp', 'ctx', None, 'grp'), may hold values from -6 to 6
- short_w: float32 [3, 3, 4096], P(None, None, 'grp'), may hold values from -2.5 to 2.5
- medium_h: bfloat16 [256, 128], P('grp'), may hold values from -3 to 3
- out_w: bfloat16 [4096, 4096], P('ctx', 'grp'), may hold values from -0.09375 to 0.09375
- grad_out: bfloat16 [4, 8192, 4096], P('dp', 'ctx', 'grp'), may hold values from -6 to 6
Outputs:
- block_out: bfloat16 [4, 8192, 4096], P('dp', 'ctx', 'grp')
- grad_projected: bfloat16 [4, 8192, 3, 4096], P('dp', 'ctx', None, 'grp')
- filter_grad: float32 [256, 128], P('grp')
- short_grad: float32 [3, 3, 4096], P(None, None, 'grp')
All inputs are finite; a program needn't handle non-finite values.
Results may differ from a plain program's by a relative error of at most 0.0064.
Values may be sent and summed in bfloat16 or wider, within the bound.
A program may use at most 128 MiB of HBM per device.

v0:
```python
import math
import jax
import jax.numpy as jnp
from jax import lax
from jax.sharding import PartitionSpec as P


def from_behind(block, axis, distance):
    devices = range(lax.axis_size(axis))
    route = [(i - distance, i) for i in devices if i - distance in devices]
    return lax.ppermute(block, axis, route)


def windows(padded, block_rows, reach):
    seqs_here = padded.shape[0]
    block_count = (padded.shape[1] - reach) // block_rows
    extended = jnp.pad(padded, ((0, 0), (0, block_rows - reach), (0, 0), (0, 0)))
    leading = extended[:, : block_count * block_rows].reshape(
        seqs_here, block_count, block_rows, padded.shape[2], padded.shape[3]
    )
    second = extended[:, block_rows:].reshape(
        seqs_here, block_count, block_rows, padded.shape[2], padded.shape[3]
    )[:, :, :reach]
    return jnp.concatenate([leading, second], axis=2)


def banded(filters, block_rows):
    groups_here = filters.shape[0]
    tap_count = filters.shape[1]
    line_width = block_rows + tap_count
    padded_line = jnp.concatenate(
        [filters, jnp.zeros((groups_here, block_rows), filters.dtype)], axis=1
    )
    tiled = jnp.broadcast_to(
        padded_line[:, None, :], (groups_here, block_rows, line_width)
    ).reshape(groups_here, block_rows * line_width)
    return tiled[:, : block_rows * (line_width - 1)].reshape(
        groups_here, block_rows, line_width - 1
    )


def band_conv(turned, matrix, block_rows):
    reach = matrix.shape[2] - block_rows
    windowed = windows(turned, block_rows, reach)
    result = jnp.einsum("gtj,sbjcg->sbtcg", matrix, windowed, preferred_element_type=jnp.float32)
    result = jnp.swapaxes(result, 3, 4)
    return result.reshape(
        turned.shape[0], turned.shape[1] - reach, turned.shape[2] * turned.shape[3]
    )


def lag_sums(grad_blocks, windowed, tap_count):
    products = jnp.einsum(
        "sbtcg,sbjcg->gtj", grad_blocks, windowed, preferred_element_type=jnp.float32
    )
    groups_here = products.shape[0]
    block_rows = products.shape[1]
    line_width = products.shape[2]
    flat_rows = jnp.pad(
        products.reshape(groups_here, block_rows * line_width), ((0, 0), (0, block_rows))
    )
    skewed = flat_rows.reshape(groups_here, block_rows, line_width + 1)[:, :, :tap_count]
    return jnp.sum(skewed, axis=1)[:, ::-1]


def featurize(padded, weights):
    short_reach = weights.shape[1] - 1
    row_count = padded.shape[1] - short_reach
    total = None
    for offset in range(weights.shape[1]):
        start = short_reach - offset
        term = weights[:, offset, :] * padded[:, start : start + row_count]
        total = term if total is None else total + term
    return total


def adjoint(padded, weights):
    short_reach = weights.shape[1] - 1
    row_count = padded.shape[1] - short_reach
    total = None
    for offset in range(weights.shape[1]):
        term = weights[:, offset, :] * padded[:, offset : offset + row_count]
        total = term if total is None else total + term
    return total


def short_sums(feature_grad, padded, short_taps):
    row_count = feature_grad.shape[1]
    short_reach = short_taps - 1
    terms = []
    for offset in range(short_taps):
        start = short_reach - offset
        terms.append(jnp.sum(feature_grad * padded[:, start : start + row_count], axis=(0, 1)))
    return jnp.stack(terms, axis=1)


def shards(projected, short_w, medium_h, out_w, grad_out):
    seq_local = projected.shape[0]
    row_count = projected.shape[1]
    chan_local = projected.shape[3]
    tap_count = medium_h.shape[1]
    reach = tap_count - 1
    short_taps = short_w.shape[1]
    short_reach = short_taps - 1
    group_local = medium_h.shape[0]
    group_size = chan_local // group_local
    block_rows = math.gcd(row_count, 128)
    front_rows = from_behind(projected[:, row_count - short_reach :], "ctx", 1)
    padded_input = jnp.concatenate([front_rows, projected], axis=1)
    features = featurize(padded_input.astype(jnp.float32), short_w)
    product = (features[:, :, 1] * features[:, :, 2]).astype(jnp.bfloat16)
    product_front = from_behind(product[:, row_count - reach :], "ctx", 1)
    product_pad = jnp.concatenate([product_front, product], axis=1)
    query = features[:, :, 0]
    keys = features[:, :, 1]
    values = features[:, :, 2]
    product_turned = jnp.swapaxes(
        product_pad.reshape(seq_local, row_count + reach, group_local, group_size), 2, 3
    )
    mixed = band_conv(product_turned, banded(medium_h[:, ::-1], block_rows), block_rows)
    gated = (query * mixed).astype(jnp.bfloat16)
    whole_gated = lax.all_gather(gated, "grp", axis=2, tiled=True)
    flat_gated = whole_gated.reshape(seq_local * row_count, whole_gated.shape[2])
    flat_cotangent = grad_out.reshape(seq_local * row_count, chan_local)
    projected_out = jnp.dot(
        flat_gated,
        lax.all_gather(out_w, "ctx", axis=0, tiled=True),
        preferred_element_type=jnp.float32,
    )
    block_out = projected_out.astype(jnp.bfloat16).reshape(seq_local, row_count, chan_local)
    input_part = lax.dot_general(
        flat_cotangent,
        lax.all_gather(out_w, "ctx", axis=0, tiled=True),
        (((1,), (1,)), ((), ())),
        preferred_element_type=jnp.float32,
    )
    summed = lax.psum_scatter(input_part, "grp", scatter_dimension=1, tiled=True)
    gated_grad = (
        lax.optimization_barrier(summed.astype(jnp.bfloat16))
        .astype(jnp.float32)
        .reshape(seq_local, row_count, chan_local)
    )
    query_grad = gated_grad * mixed
    mix_grad = (gated_grad * query).astype(jnp.bfloat16)
    mix_back = from_behind(mix_grad[:, :reach], "ctx", -1)
    mix_turned = jnp.swapaxes(
        jnp.concatenate([mix_grad, mix_back], axis=1).reshape(
            seq_local, row_count + reach, group_local, group_size
        ),
        2,
        3,
    )
    product_grad = band_conv(mix_turned, banded(medium_h, block_rows), block_rows)
    grad_blocks = jnp.swapaxes(
        mix_grad.reshape(seq_local, row_count // block_rows, block_rows, group_local, group_size),
        3,
        4,
    )
    filter_part = lag_sums(grad_blocks, windows(product_turned, block_rows, reach), tap_count)
    feature_grad = jnp.stack(
        [query_grad, product_grad * values, product_grad * keys], axis=2
    ).astype(jnp.bfloat16)
    grad_back = from_behind(feature_grad[:, :short_reach], "ctx", -1)
    grad_pad = jnp.concatenate([feature_grad, grad_back], axis=1).astype(jnp.float32)
    grad_projected = adjoint(grad_pad, short_w).astype(jnp.bfloat16)
    short_part = short_sums(
        feature_grad.astype(jnp.float32), padded_input.astype(jnp.float32), short_taps
    )
    filter_total, short_total = lax.psum((filter_part, short_part), ("dp", "ctx"))
    seq_total = seq_local * lax.axis_size("dp")
    length_total = row_count * lax.axis_size("ctx")
    filter_grad = filter_total / math.sqrt(seq_total * length_total * group_size)
    short_grad = short_total / math.sqrt(seq_total * length_total)
    return (block_out, grad_projected, filter_grad, short_grad)


def solution(mesh):
    in_specs = (
        P("dp", "ctx", None, "grp"),
        P(None, None, "grp"),
        P("grp", None),
        P("ctx", "grp"),
        P("dp", "ctx", "grp"),
    )
    out_specs = (
        P("dp", "ctx", "grp"),
        P("dp", "ctx", None, "grp"),
        P("grp", None),
        P(None, None, "grp"),
    )
    return jax.shard_map(shards, mesh=mesh, in_specs=in_specs, out_specs=out_specs, check_vma=False)
```

profile of v0, /device:TPU:1, one launch (start us, length us, event | category | flops | bytes accessed | tf_op | source)
XLA Modules:
  0.0 600.7 jit_solution(14814459723128327061)
XLA Ops:
  8.0 103.6 %all-gather.5.cloned.1.call-done = bf16[4096,1024]{1,0:T(8,128)(2,1)} async-done(((bf16[128,1024]{1,0:T(8,128)(2,1)}), bf16[4096,1024]{1,0:T(8,128)(2,1)}) %all-gather.5.cloned.1.call-update) | async-done | bytes 8388624 | tf_op jit(solution)/shard_map/all_gather | solution.py:127
  111.5 10.1 %fusion.31 = f32[512,4096]{1,0:T(8,128)} fusion(bf16[512,1024]{1,0:T(8,128)(2,1)S(1)} %bitcast.91, bf16[4096,1024]{1,0:T(8,128)(2,1)} %all-gather.5.cloned.1.call-done), kind=kOutput, calls=%fused_computation.57 | convolution fusion | flops 4294967296 | bytes 17825792 | tf_op jit(solution)/shard_map/dot_general | solution.py:131
  124.5 4.6 copy.57
  130.0 4.6 maximum_convert_fusion
  138.3 5.9 multiply_add_fusion
  144.2 58.5 %reduce-scatter.2.cloned.1.call-done = f32[512,1024]{1,0:T(8,128)} async-done(((f32[512,4096]{1,0:T(8,128)}), f32[512,1024]{1,0:T(8,128)}) %reduce-scatter.2.cloned.1.call-update) | async-done | bytes 2097168 | tf_op jit(solution)/shard_map/reduce_scatter | solution.py:137
  216.5 15.8 %reshape.121 = bf16[64,128,255,1,1]{2,1,0,3,4:T(8,128)(2,1)} reshape(bf16[64,32640]{1,0:T(8,128)(2,1)} %slice.126) | data formatting | bytes 8355840 | tf_op jit(solution)/shard_map/reshape | solution.py:37
  243.7 4.1 fusion.20
  250.3 3.9 reshape.116
  254.1 5.9 multiply_convert_fusion.1
  262.1 4.8 collective-permute-start.1
  272.2 16.0 %reshape.120 = bf16[64,128,255,1,1]{2,1,0,3,4:T(8,128)(2,1)} reshape(bf16[64,32640]{1,0:T(8,128)(2,1)} %slice.122) | data formatting | bytes 8355840 | tf_op jit(solution)/shard_map/reshape | solution.py:37
  297.5 3.9 fusion.26
  308.1 3.7 fusion.17
  318.7 6.2 %convolution_bitcast_fusion = f32[64,128,255]{2,1,0:T(8,128)} fusion(bf16[2,2,255,16,64]{2,3,1,0,4:T(8,128)(2,1)} %copy-done.5, bf16[2,2,128,16,64]{2,1,0,3,4:T(2,128)(2,1)S(1)} %copy-done.9), kind=kOutput, calls=%fused_computation.20 | convolution fusion | flops 267386880 | bytes 11493376 | tf_op jit(solution)/shard_map/sbtcg,sbjcg->gtj/dot_general | solution.py:53
  324.9 9.2 %reshape.118 = f32[64,32640]{1,0:T(8,128)} reshape(f32[64,128,255]{2,1,0:T(8,128)} %convolution_bitcast_fusion) | data formatting | bytes 16711680 | tf_op jit(solution)/shard_map/reshape | solution.py:60
  334.1 4.0 pad.16
  344.4 10.9 %fusion = (f32[3,1024]{1,0:T(4,128)S(1)}, f32[3,1024]{1,0:T(4,128)S(1)}, f32[3,1024]{1,0:T(4,128)S(1)}) fusion(f32[2,258,3,1024]{1,3,0,2:T(8,128)} %copy-done.2, bf16[2,256,1,1024]{1,3,0,2:T(8,128)(2,1)S(1)} %copy-done.4, bf16[2,256,1,1024]{1,3,0,2:T(8,128)(2,1)S(1)} %copy-done.3, bf16[2,256,1,1024]{1,3,0,2:T(8,128)(2,1)S(1)} %multiply_convert_fusion.2), kind=kLoop, calls=%fused_computation.3 | loop fusion | flops 14146560 | bytes 22056960 | tf_op jit(solution)/shard_map/reduce_sum | solution.py:93
  371.8 5.8 fusion.4
  377.6 4.6 copy.78
  382.2 145.3 %all-reduce.8.cloned.1.call-done = (f32[64,128]{1,0:T(8,128)}, f32[3,3,1024]{2,0,1:T(4,128)}) async-done(((f32[64,128]{1,0:T(8,128)}, f32[3,3,1024]{2,0,1:T(4,128)}), (f32[64,128]{1,0:T(8,128)}, f32[3,3,1024]{2,0,1:T(4,128)})) %all-reduce.8.cloned.1.call-update) | async-done | bytes 69648 | tf_op jit(solution)/shard_map/psum | solution.py:169
  530.4 46.8 %all-gather.3.cloned.1.call-done = bf16[2,256,4096]{1,2,0:T(8,128)(2,1)} async-done(((bf16[2,256,1024]{1,2,0:T(8,128)(2,1)}), bf16[2,256,4096]{1,2,0:T(8,128)(2,1)}) %all-gather.3.cloned.1.call-update) | async-done | bytes 4194320 | tf_op jit(solution)/shard_map/all_gather | solution.py:122
  577.3 6.5 %copy.63 = bf16[2,256,4096]{2,1,0:T(8,128)(2,1)} copy(bf16[2,256,4096]{1,2,0:T(8,128)(2,1)} %all-gather.3.cloned.1.call-done) | data formatting | bytes 8388608 | tf_op jit(solution)/shard_map/all_gather | solution.py:122
  583.8 10.2 %convolution_convert_fusion = bf16[512,1024]{1,0:T(8,128)(2,1)} fusion(bf16[512,4096]{1,0:T(8,128)(2,1)} %bitcast.102, bf16[4096,1024]{1,0:T(8,128)(2,1)} %all-gather.5.cloned.1.call-done), kind=kOutput, calls=%fused_computation.42 | convolution fusion | flops 4295491584 | bytes 13631488 | tf_op jit(solution)/shard_map/dot_general | solution.py:125
  (93 shorter events, 91.3 us)
Async XLA Ops:
  7.2 104.4 %copy-start = (bf16[2,256,1024]{2,1,0:T(8,128)(2,1)S(1)}, bf16[2,256,1024]{2,1,0:T(8,128)(2,1)}, u32[]{:S(2)}) copy-start(bf16[2,256,1024]{2,1,0:T(8,128)(2,1)} %param.9) | copy-start | bytes 3145732
  7.2 104.3 %all-gather.5.cloned.1.call-start = ((), (), s32[]{:S(2)}) async-start(), calls=%async_computation.2 | async-start | bytes 8650752 | tf_op jit(solution)/shard_map/all_gather | solution.py:127
  7.9 194.7 %reduce-scatter.2.cloned.1.call-start = ((), (), s32[]{:S(2)}) async-start(), calls=%async_computation.3 | async-start | bytes 10485760 | tf_op jit(solution)/shard_map/reduce_scatter | solution.py:137
  121.7 2.8 copy-start.11
  121.7 405.9 %all-reduce.8.cloned.1.call-start = ((), (), s32[]{:S(2)}) async-start(), calls=%async_computation.4 | async-start | bytes 163840 | tf_op jit(solution)/shard_map/psum | solution.py:169
  122.7 6.5 %collective-permute-start = (bf16[2,2,3,1024]{3,1,2,0:T(2,128)(2,1)S(1)}, bf16[2,2,3,1024]{3,1,2,0:T(2,128)(2,1)S(1)}, u32[]{:S(2)}, u32[]{:S(2)}) collective-permute-start(bf16[2,2,3,1024]{3,1,2,0:T(2,128)(2,1)S(1)} %slice.89), channel_id=1, source_target_pairs={{0,4},{4,8},{8,12},{12,16},{16,20},{20,24},{24,28},{28,32},{32,36}... | collective-permute-start | bytes 73736 | tf_op jit(solution)/shard_map/ppermute | solution.py:11
  134.6 3.7 copy-start.2
  206.4 4.8 copy-start.10
  208.9 2.4 copy-start.6
  209.8 22.5 %collective-permute-start.2 = (bf16[2,127,1024]{1,2,0:T(8,128)(2,1)}, bf16[2,127,1024]{1,2,0:T(8,128)(2,1)}, u32[]{:S(2)}, u32[]{:S(2)}) collective-permute-start(bf16[2,127,1024]{1,2,0:T(8,128)(2,1)} %slice.123), channel_id=1, source_target_pairs={{4,0},{8,4},{12,8},{16,12},{20,16},{24,20},{28,24},{32,28},{36,32}... | collective-permute-start | bytes 1560584 | tf_op jit(solution)/shard_map/ppermute | solution.py:11
  260.1 1.0 copy-start.7
  262.1 39.3 %collective-permute-start.1 = (bf16[2,127,1024]{1,2,0:T(8,128)(2,1)}, bf16[2,127,1024]{1,2,0:T(8,128)(2,1)}, u32[]{:S(2)}, u32[]{:S(2)}) collective-permute-start(bf16[2,127,1024]{1,2,0:T(8,128)(2,1)} %slice.119), channel_id=1, source_target_pairs={{0,4},{4,8},{8,12},{12,16},{16,20},{20,24},{24,28},{28,32},{32,36}... | collective-permute-start | bytes 1560584 | tf_op jit(solution)/shard_map/ppermute | solution.py:11
  297.5 3.9 copy-start.8
  306.7 1.3 copy-start.5
  315.6 3.0 copy-start.9
  341.2 3.2 copy-start.3
  341.2 3.2 copy-start.4
  355.9 221.4 %all-gather.3.cloned.1.call-start = ((), (), s32[]{:S(2)}) async-start(), calls=%async_computation.1 | async-start | bytes 5242880 | tf_op jit(solution)/shard_map/all_gather | solution.py:122
  362.9 4.6 collective-permute-start.3
  583.8 10.2 %copy-start.1 = (bf16[2,256,1024]{2,1,0:T(8,128)(2,1)S(1)}, bf16[2,256,1024]{2,1,0:T(8,128)(2,1)}, u32[]{:S(2)}) copy-start(bf16[2,256,1024]{2,1,0:T(8,128)(2,1)} %param.9) | copy-start | bytes 3145732
Sparse Core Ops, SparseCore 0:
  10.6 100.9 all-gather.4
  121.8 80.7 reduce-scatter.1
  356.0 171.5 all-reduce.7
  529.8 47.3 all-gather.2
where the time goes:
time: 607 us; the launch traced here: 601 us
  waiting for transfers between devices  358 us (59%)
  local copies, waits for them, and re-layouts  127 us (21%)
  other arithmetic  56.9 us (9%)
  matrix products  34.4 us (6%)
  between operations  14.3 us (2%)
  starting transfers between devices  9.42 us (2%)
    psum x1, waiting for transfers between devices, shards(): lax.psum((filter_part, short_part), ('dp', 'ctx'))  145 us
    all_gather x1, waiting for transfers between devices, shards(): lax.all_gather(out_w, 'ctx', axis=0, tiled=True)  104 us
    reduce_scatter x1, waiting for transfers between devices, shards(): lax.psum_scatter(input_part, 'grp', scatter_dimension=1, tiled=True)  58.5 us
    all_gather x1, waiting for transfers between devices, shards(): whole_gated = lax.all_gather(gated, 'grp', axis=2, tiled=True)  46.8 us
    reshape x2, local copies, waits for them, and re-layouts, banded(): tiled[:, :block_rows * (line_width - 1)]  31.8 us
    unnamed x34, local copies, waits for them, and re-layouts  25.5 us
  transfers between devices with their start and end apart: 8, of which 5 were waited for; matrix products, arithmetic and copies ran while one was open for 16% of the time, Pallas kernels for 0%

commit v1 on v0

--- a/solution.py
+++ b/solution.py
@@ -3,6 +3,11 @@
 import jax.numpy as jnp
 from jax import lax
 from jax.sharding import PartitionSpec as P
+
+
+def gather_over(block, name, d):
+    stack = jnp.stack([block] * lax.axis_size(name))
+    return jnp.concatenate(lax.all_to_all(stack, name, 0, 0), axis=d)
 
 
 def from_behind(block, axis, distance):
@@ -123,9 +128,7 @@
     flat_gated = whole_gated.reshape(seq_local * row_count, whole_gated.shape[2])
     flat_cotangent = grad_out.reshape(seq_local * row_count, chan_local)
     projected_out = jnp.dot(
-        flat_gated,
-        lax.all_gather(out_w, "ctx", axis=0, tiled=True),
-        preferred_element_type=jnp.float32,
+        flat_gated, gather_over(out_w, "ctx", 0), preferred_element_type=jnp.float32
     )
     block_out = projected_out.astype(jnp.bfloat16).reshape(seq_local, row_count, chan_local)
     input_part = lax.dot_general(

time: 607 us -> 738 us (1.22)
  waiting for transfers between devices: 358 us -> 478 us
  starting transfers between devices: 9.42 us -> 17.5 us
    ppermute x4, waiting for transfers between devices: 3.28 us -> 174 us  [from_behind(): return lax.ppermute(block, axis, route)]
    reduce_scatter x1, waiting for transfers between devices: 58.5 us -> 0.01 us  [shards(): lax.psum_scatter(input_part, 'grp', scatter_dimension=1, tiled=True)]
    psum x1, waiting for transfers between devices: 145 us -> 153 us  [shards(): lax.psum((filter_part, short_part), ('dp', 'ctx'))]
    unnamed x34 -> x40, local copies, waits for them, and re-layouts: 25.5 us -> 26.5 us
  transfers between devices with their start and end apart: 8 -> 9, of which waited for: 5 -> 5; matrix products, arithmetic and copies ran while one was open for 16% -> 26% of each run, Pallas kernels for 0% -> 0%
where the time goes in v1:
time: 738 us; the launch traced here: 730 us
  waiting for transfers between devices  478 us (65%)
  local copies, waits for them, and re-layouts  132 us (18%)
  other arithmetic  55.9 us (8%)
  matrix products  32.1 us (4%)
  starting transfers between devices  17.5 us (2%)
  between operations  14.3 us (2%)
    ppermute x4, waiting for transfers between devices, from_behind(): return lax.ppermute(block, axis, route)  174 us
    psum x1, waiting for transfers between devices, shards(): lax.psum((filter_part, short_part), ('dp', 'ctx'))  153 us
    all_gather x1, waiting for transfers between devices, shards(): lax.all_gather(out_w, 'ctx', axis=0, tiled=True)  104 us
    all_gather x1, waiting for transfers between devices, shards(): whole_gated = lax.all_gather(gated, 'grp', axis=2, tiled=True)  46.8 us
    reshape x2, local copies, waits for them, and re-layouts, banded(): tiled[:, :block_rows * (line_width - 1)]  32 us
    unnamed x40, local copies, waits for them, and re-layouts  26.5 us
  transfers between devices with their start and end apart: 9, of which 5 were waited for; matrix products, arithmetic and copies ran while one was open for 26% of the time, Pallas kernels for 0%

profile of v1, /device:TPU:1, one launch (start us, length us, event | category | flops | bytes accessed | tf_op | source)
XLA Modules:
  0.0 730.0 jit_solution(5225025767518684361)
XLA Ops:
  8.0 103.6 %all-gather.5.cloned.1.call-done = bf16[4096,1024]{1,0:T(8,128)(2,1)} async-done(((bf16[128,1024]{1,0:T(8,128)(2,1)}), bf16[4096,1024]{1,0:T(8,128)(2,1)}) %all-gather.5.cloned.1.call-update) | async-done | bytes 8388624 | tf_op jit(solution)/shard_map/all_gather | solution.py:136
  111.5 10.1 %fusion.31 = f32[512,4096]{1,0:T(8,128)} fusion(bf16[512,1024]{1,0:T(8,128)(2,1)S(1)} %bitcast.92, bf16[4096,1024]{1,0:T(8,128)(2,1)} %all-gather.5.cloned.1.call-done), kind=kOutput, calls=%fused_computation.57 | convolution fusion | flops 4294967296 | bytes 17825792 | tf_op jit(solution)/shard_map/dot_general | solution.py:134
  122.6 4.4 stack.13
  127.0 5.6 all-to-all-start
  136.7 4.6 copy.57
  141.4 170.7 %collective-permute-done = bf16[2,2,3,1024]{3,1,2,0:T(2,128)(2,1)S(1)} collective-permute-done((bf16[2,2,3,1024]{3,1,2,0:T(2,128)(2,1)S(1)}, bf16[2,2,3,1024]{3,1,2,0:T(2,128)(2,1)S(1)}, u32[]{:S(2)}, u32[]{:S(2)}) %collective-permute-start) | collective-permute-done | bytes 24608 | tf_op jit(solution)/shard_map/ppermute | solution.py:16
  312.9 3.8 maximum_convert_fusion
  320.4 5.9 multiply_add_fusion
  340.1 15.9 %reshape.127 = bf16[64,128,255,1,1]{2,1,0,3,4:T(8,128)(2,1)} reshape(bf16[64,32640]{1,0:T(8,128)(2,1)} %slice.126) | data formatting | bytes 8355840 | tf_op jit(solution)/shard_map/reshape | solution.py:42
  367.4 4.1 fusion.20
  373.9 3.9 reshape.122
  377.8 5.9 multiply_convert_fusion.1
  385.7 6.0 collective-permute-start.1
  396.9 16.1 %reshape.126 = bf16[64,128,255,1,1]{2,1,0,3,4:T(8,128)(2,1)} reshape(bf16[64,32640]{1,0:T(8,128)(2,1)} %slice.122) | data formatting | bytes 8355840 | tf_op jit(solution)/shard_map/reshape | solution.py:42
  440.4 6.2 convolution_bitcast_fusion
  446.5 9.3 %reshape.124 = f32[64,32640]{1,0:T(8,128)} reshape(f32[64,128,255]{2,1,0:T(8,128)} %convolution_bitcast_fusion) | data formatting | bytes 16711680 | tf_op jit(solution)/shard_map/reshape | solution.py:65
  455.8 4.0 pad.16
  466.0 10.8 %fusion = (f32[3,1024]{1,0:T(4,128)S(1)}, f32[3,1024]{1,0:T(4,128)S(1)}, f32[3,1024]{1,0:T(4,128)S(1)}) fusion(f32[2,258,3,1024]{1,3,0,2:T(8,128)} %copy-done.2, bf16[2,256,1,1024]{1,3,0,2:T(8,128)(2,1)S(1)} %copy-done.5, bf16[2,256,1,1024]{1,3,0,2:T(8,128)(2,1)S(1)} %copy-done.4, bf16[2,256,1,1024]{1,3,0,2:T(8,128)(2,1)S(1)} %multiply_convert_fusion.2), kind=kLoop, calls=%fused_computation.3 | loop fusion | flops 14146560 | bytes 22056960 | tf_op jit(solution)/shard_map/reduce_sum | solution.py:98
  493.6 5.8 fusion.4
  499.4 4.6 copy.78
  504.0 152.9 %all-reduce.8.cloned.1.call-done = (f32[64,128]{1,0:T(8,128)}, f32[3,3,1024]{2,0,1:T(4,128)}) async-done(((f32[64,128]{1,0:T(8,128)}, f32[3,3,1024]{2,0,1:T(4,128)}), (f32[64,128]{1,0:T(8,128)}, f32[3,3,1024]{2,0,1:T(4,128)})) %all-reduce.8.cloned.1.call-update) | async-done | bytes 69648 | tf_op jit(solution)/shard_map/psum | solution.py:172
  659.8 46.8 %all-gather.3.cloned.1.call-done = bf16[2,256,4096]{1,2,0:T(8,128)(2,1)} async-done(((bf16[2,256,1024]{1,2,0:T(8,128)(2,1)}), bf16[2,256,4096]{1,2,0:T(8,128)(2,1)}) %all-gather.3.cloned.1.call-update) | async-done | bytes 4194320 | tf_op jit(solution)/shard_map/all_gather | solution.py:127
  706.6 6.5 copy.63
  713.1 10.2 %convolution_convert_fusion = bf16[512,1024]{1,0:T(8,128)(2,1)} fusion(bf16[512,4096]{1,0:T(8,128)(2,1)} %bitcast.103, bf16[4096,1024]{1,0:T(8,128)(2,1)} %bitcast.8), kind=kOutput, calls=%fused_computation.42 | convolution fusion | flops 4295491584 | bytes 13631488 | tf_op jit(solution)/shard_map/dot_general | solution.py:130
  (102 shorter events, 98.0 us)
Async XLA Ops:
  7.2 104.4 %copy-start = (bf16[2,256,1024]{2,1,0:T(8,128)(2,1)S(1)}, bf16[2,256,1024]{2,1,0:T(8,128)(2,1)}, u32[]{:S(2)}) copy-start(bf16[2,256,1024]{2,1,0:T(8,128)(2,1)} %param.9) | copy-start | bytes 3145732
  7.2 104.3 %all-gather.5.cloned.1.call-start = ((), (), s32[]{:S(2)}) async-start(), calls=%async_computation.3 | async-start | bytes 8650752 | tf_op jit(solution)/shard_map/all_gather | solution.py:136
  7.9 318.4 %reduce-scatter.2.cloned.1.call-start = ((), (), s32[]{:S(2)}) async-start(), calls=%async_computation.4 | async-start | bytes 10485760 | tf_op jit(solution)/shard_map/reduce_scatter | solution.py:140
  121.6 0.9 copy-start.12
  127.0 9.7 %copy-start.14 = (f32[3,3,1024]{2,1,0:T(4,128)S(1)}, f32[3,3,1024]{2,1,0:T(4,128)}, u32[]{:S(2)}) copy-start(f32[3,3,1024]{2,1,0:T(4,128)} %param.6) | copy-start | bytes 110596
  127.0 586.1 %all-to-all-start = ((bf16[32,128,1024]{2,1,0:T(8,128)(2,1)}), bf16[32,128,1024]{2,1,0:T(8,128)(2,1)}, u32[]{:S(2)}, u32[]{:S(2)}) async-start(bf16[32,128,1024]{2,1,0:T(8,128)(2,1)} %stack.13), calls=%async_computation | async-start | bytes 16777216 | tf_op jit(solution)/shard_map/all_to_all | solution.py:10
  132.6 524.3 %all-reduce.8.cloned.1.call-start = ((), (), s32[]{:S(2)}) async-start(), calls=%async_computation.5 | async-start | bytes 163840 | tf_op jit(solution)/shard_map/psum | solution.py:172
  133.6 178.5 %collective-permute-start = (bf16[2,2,3,1024]{3,1,2,0:T(2,128)(2,1)S(1)}, bf16[2,2,3,1024]{3,1,2,0:T(2,128)(2,1)S(1)}, u32[]{:S(2)}, u32[]{:S(2)}) collective-permute-start(bf16[2,2,3,1024]{3,1,2,0:T(2,128)(2,1)S(1)} %slice.89), channel_id=1, source_target_pairs={{0,4},{4,8},{8,12},{12,16},{16,20},{20,24},{24,28},{28,32},{32,36}... | collective-permute-start | bytes 73736 | tf_op jit(solution)/shard_map/ppermute | solution.py:16
  316.7 3.7 copy-start.2
  330.1 4.8 copy-start.13
  332.6 2.4 copy-start.8
  333.5 22.5 %collective-permute-start.2 = (bf16[2,127,1024]{1,2,0:T(8,128)(2,1)}, bf16[2,127,1024]{1,2,0:T(8,128)(2,1)}, u32[]{:S(2)}, u32[]{:S(2)}) collective-permute-start(bf16[2,127,1024]{1,2,0:T(8,128)(2,1)} %slice.123), channel_id=1, source_target_pairs={{4,0},{8,4},{12,8},{16,12},{20,16},{24,20},{28,24},{32,28},{36,32}... | collective-permute-start | bytes 1560584 | tf_op jit(solution)/shard_map/ppermute | solution.py:16
  383.7 1.0 copy-start.9
  385.7 41.4 %collective-permute-start.1 = (bf16[2,127,1024]{1,2,0:T(8,128)(2,1)}, bf16[2,127,1024]{1,2,0:T(8,128)(2,1)}, u32[]{:S(2)}, u32[]{:S(2)}) collective-permute-start(bf16[2,127,1024]{1,2,0:T(8,128)(2,1)} %slice.119), channel_id=1, source_target_pairs={{0,4},{4,8},{8,12},{12,16},{16,20},{20,24},{24,28},{28,32},{32,36}... | collective-permute-start | bytes 1560584 | tf_op jit(solution)/shard_map/ppermute | solution.py:16
  419.9 3.4 copy-start.7
  419.9 7.2 copy-start.10
  429.7 2.2 copy-start.3
  431.9 1.6 copy-start.6
  434.6 5.7 copy-start.11
  462.3 3.7 copy-start.4
  462.3 3.7 copy-start.5
  477.5 229.1 %all-gather.3.cloned.1.call-start = ((), (), s32[]{:S(2)}) async-start(), calls=%async_computation.2 | async-start | bytes 5242880 | tf_op jit(solution)/shard_map/all_gather | solution.py:127
  484.5 4.8 collective-permute-start.3
  713.1 10.2 %copy-start.1 = (bf16[2,256,1024]{2,1,0:T(8,128)(2,1)S(1)}, bf16[2,256,1024]{2,1,0:T(8,128)(2,1)}, u32[]{:S(2)}) copy-start(bf16[2,256,1024]{2,1,0:T(8,128)(2,1)} %param.9) | copy-start | bytes 3145732
Sparse Core Ops, SparseCore 0:
  10.6 100.9 all-gather.4
  121.8 80.7 reduce-scatter.1
  477.6 179.2 all-reduce.7
  659.2 47.3 all-gather.2
